TPU v7x, 32 devices: a whole 2x2x4 slice. The times are simulated.
32 devices in a mesh: dp: 4 (over y, x), seq: 2 (over core), tensor: 4 (over z).
Axes of the slice: x: 2, y: 2, z: 4, core: 2. Of those that a mesh axis runs over, the one named last changes fastest.
Arguments:
- block_input: float32 [4, 16, 256, 1024], P('dp', 'seq', 'tensor'), may hold values from -6 to 6
- w_qkv: bfloat16 [1024, 3, 1024], P(None, None, 'tensor'), may hold values from -0.1875 to 0.1875
- qv_bias: bfloat16 [2, 1024], P(None, 'tensor'), may hold values from -3 to 3
- w_out: bfloat16 [1024, 1024], P('tensor'), may hold values from -3 to 3
- b_out: bfloat16 [1024], replicated, may hold values from -3 to 3
- w_up: bfloat16 [1024, 4096], P(None, 'tensor'), may hold values from -0.1875 to 0.1875
- b_up: bfloat16 [4096], P('tensor'), may hold values from -3 to 3
- w_down: bfloat16 [4096, 1024], P('tensor'), may hold values from -0.09375 to 0.09375
- b_down: bfloat16 [1024], replicated, may hold values from -3 to 3
- w_mod: bfloat16 [1024, 6144], replicated, may hold values from -0.375 to 0.375
- b_mod: bfloat16 [6144], replicated, may hold values from -3 to 3
- context_frames: int32 [4], P('dp'), may hold values from 1 to 15
- noise_levels: int32 [4, 16], P('dp', 'seq'), may hold values from 0 to 999
- cotangent: float32 [4, 16, 256, 1024], P('dp', 'seq', 'tensor'), may hold values from -6 to 6
Outputs:
- output: float32 [4, 16, 256, 1024], P('dp', 'seq', 'tensor')
- grad_input: float32 [4, 16, 256, 1024], P('dp', 'seq', 'tensor')
- grad_w_qkv: float32 [1024, 3, 1024], P(None, None, 'tensor')
- grad_qv_bias: float32 [2, 1024], P(None, 'tensor')
- grad_w_out: float32 [1024, 1024], P('tensor')
- grad_b_out: float32 [1024], P('tensor')
- grad_w_up: float32 [1024, 4096], P(None, 'tensor')
- grad_b_up: float32 [4096], P('tensor')
- grad_w_down: float32 [4096, 1024], P('tensor')
- grad_b_down: float32 [1024], P('tensor')
- grad_w_mod: float32 [1024, 6144], P(None, 'tensor')
- grad_b_mod: float32 [6144], P('tensor')
Inputs may be any that keep to these rules, and one draw needn't show every extreme that they name: `noise_levels`: noise level index of each frame.
All inputs are finite; a program needn't handle non-finite values.
Results may differ from a plain program's by a relative error of at most 0.02.
Values may be sent and summed in bfloat16 or wider, within the bound.
No kernel may reach another device: no remote copies, remote signals or barrier semaphores. Data moves between devices by JAX's collectives and lax.ppermute only.
A program may use at most 256 MiB of HBM per device.

v0:
```python
import math
import jax
import jax.numpy as jnp
from jax import lax
from jax.sharding import PartitionSpec as P

HD = 64


def level_features(levels, context, frame_ids, breadth):
    level_used = jnp.where(frame_ids[None, :] < context[:, None], 0, levels).astype(jnp.float32)
    halfway = breadth // 2
    frequency = jnp.exp(-math.log(10000.0) * jnp.arange(halfway, dtype=jnp.float32) / halfway)
    angles = level_used[..., None] * frequency
    return jax.nn.silu(jnp.concatenate([jnp.cos(angles), jnp.sin(angles)], axis=-1))


def normalize(stream):
    centre = stream - jnp.mean(stream, axis=-1, keepdims=True)
    inverse = lax.rsqrt(jnp.mean(centre * centre, axis=-1, keepdims=True) + 1e-06)
    return (centre * inverse, inverse)


def norm_back(grad_normed, normed, inverse):
    first_mean = jnp.mean(grad_normed, axis=-1, keepdims=True)
    second_mean = jnp.mean(grad_normed * normed, axis=-1, keepdims=True)
    return inverse * (grad_normed - first_mean - normed * second_mean)


def gelu_back(pre_act, grad_act):
    _, pullback = jax.vjp(lambda argument: jax.nn.gelu(argument, approximate=True), pre_act)
    return pullback(grad_act)[0]


def body(
    block_input,
    w_qkv,
    qv_bias,
    w_out,
    b_out,
    w_up,
    b_up,
    w_down,
    b_down,
    w_mod,
    b_mod,
    context_frames,
    noise_levels,
    cotangent,
):
    clip_count, half_frames, patch_local, breadth = block_input.shape
    patches_all = patch_local * lax.axis_size("tensor")
    head_cols = w_qkv.shape[2]
    heads_local = head_cols // HD
    softmax_scale = HD ** (-0.5)
    frame_first = lax.axis_index("seq") * half_frames
    frame_ids = frame_first + jnp.arange(half_frames, dtype=jnp.int32)
    condition = level_features(noise_levels, context_frames, frame_ids, breadth).astype(
        jnp.bfloat16
    )
    modulation = jnp.einsum(
        "cfd,de->cfe", condition, w_mod, preferred_element_type=jnp.float32
    ) + b_mod.astype(jnp.float32)
    shift_one, scale_one, gate_one, shift_two, scale_two, gate_two = jnp.split(
        modulation[:, :, None, :], 6, axis=-1
    )
    normed_one, inverse_one = normalize(block_input)
    attn_in = (normed_one * (1.0 + scale_one) + shift_one).astype(jnp.bfloat16)
    attn_all = lax.all_gather(attn_in, "tensor", axis=2, tiled=True)
    projected = jnp.einsum("cfpd,dke->cfpke", attn_all, w_qkv, preferred_element_type=jnp.float32)
    bias_float = qv_bias.astype(jnp.float32)
    queries = (projected[..., 0, :] + bias_float[0]).astype(jnp.bfloat16)
    key_local = projected[..., 1, :].astype(jnp.bfloat16)
    value_local = (projected[..., 2, :] + bias_float[1]).astype(jnp.bfloat16)
    key_clip, value_clip = (
        lax.all_gather(key_local, "seq", axis=1, tiled=True),
        lax.all_gather(value_local, "seq", axis=1, tiled=True),
    )
    query_rows = half_frames * patches_all
    block_rows = min(512, query_rows)
    block_count = query_rows // block_rows
    key_rows = key_clip.shape[1] * patches_all
    key_frame = jnp.arange(key_rows, dtype=jnp.int32) // patches_all
    query_frames = (frame_first + jnp.arange(query_rows, dtype=jnp.int32) // patches_all).reshape(
        block_count, block_rows
    )
    query_heads = queries.reshape(clip_count, block_count, block_rows, heads_local, HD)
    key_heads = key_clip.reshape(clip_count, key_rows, heads_local, HD)
    value_heads = value_clip.reshape(clip_count, key_rows, heads_local, HD)

    def masked_scores(query_block, keys, frames_block, context_limit):
        scores = (
            jnp.einsum("bhd,khd->hbk", query_block, keys, preferred_element_type=jnp.float32)
            * softmax_scale
        )
        allowed = (key_frame[None, :] <= frames_block[:, None]) | (
            key_frame[None, :] < context_limit
        )
        return jnp.where(allowed[None], scores, -1e30)

    def forward_clip(members):
        clip_queries, keys, values, context_limit = members

        def forward_block(slices):
            query_block, frames_block = slices
            scores = masked_scores(query_block, keys, frames_block, context_limit)
            row_max = jnp.max(scores, axis=-1, keepdims=True)
            exponent = jnp.exp(scores - row_max)
            denominator = jnp.sum(exponent, axis=-1, keepdims=True)
            probability = (exponent / denominator).astype(jnp.bfloat16)
            result = jnp.einsum(
                "hbk,khd->bhd", probability, values, preferred_element_type=jnp.float32
            )
            return (result.astype(jnp.bfloat16), (row_max + jnp.log(denominator))[..., 0])

        return lax.map(forward_block, (clip_queries, query_frames))

    attended, log_total = lax.map(
        forward_clip, (query_heads, key_heads, value_heads, context_frames)
    )
    attended_rows = attended.reshape(clip_count, half_frames, patches_all, head_cols)
    portion = attended_rows
    branch_rows = lax.psum_scatter(
        jnp.einsum("cfpe,ed->pcfd", portion, w_out, preferred_element_type=jnp.float32).astype(
            jnp.bfloat16
        ),
        "tensor",
        scatter_dimension=0,
        tiled=True,
    ).astype(jnp.float32)
    branch_one = jnp.transpose(branch_rows, (1, 2, 0, 3)) + b_out.astype(jnp.float32)
    hidden_one = block_input + gate_one * branch_one
    normed_two, inverse_two = normalize(hidden_one)
    mlp_in = (normed_two * (1.0 + scale_two) + shift_two).astype(jnp.bfloat16)
    mlp_all = lax.all_gather(mlp_in, "tensor", axis=2, tiled=True)
    pre_act = jnp.einsum(
        "cfpd,de->cfpe", mlp_all, w_up, preferred_element_type=jnp.float32
    ) + b_up.astype(jnp.float32)
    activated = jax.nn.gelu(pre_act, approximate=True).astype(jnp.bfloat16)
    portion = activated
    mlp_rows = lax.psum_scatter(
        jnp.einsum("cfpe,ed->pcfd", portion, w_down, preferred_element_type=jnp.float32).astype(
            jnp.bfloat16
        ),
        "tensor",
        scatter_dimension=0,
        tiled=True,
    ).astype(jnp.float32)
    mlp_out = jnp.transpose(mlp_rows, (1, 2, 0, 3)) + b_down.astype(jnp.float32)
    output = hidden_one + gate_two * mlp_out
    grad_mlp = gate_two * cotangent
    grad_gate_two = jnp.sum(cotangent * mlp_out, axis=2)
    grad_b_down = jnp.sum(grad_mlp, axis=(0, 1, 2))
    grad_mlp_low = grad_mlp.astype(jnp.bfloat16)
    grad_mlp_all = lax.all_gather(grad_mlp_low, "tensor", axis=2, tiled=True)
    grad_act = jnp.einsum("cfpd,ed->cfpe", grad_mlp_all, w_down, preferred_element_type=jnp.float32)
    grad_w_down = jnp.einsum(
        "cfpe,cfpd->ed", activated, grad_mlp_all, preferred_element_type=jnp.float32
    )
    grad_pre = gelu_back(pre_act, grad_act).astype(jnp.bfloat16)
    grad_b_up = jnp.sum(grad_pre.astype(jnp.float32), axis=(0, 1, 2))
    grad_w_up = jnp.einsum("cfpd,cfpe->de", mlp_all, grad_pre, preferred_element_type=jnp.float32)
    portion = grad_pre
    grad_mlp_rows = lax.psum_scatter(
        jnp.einsum("cfpe,de->pcfd", portion, w_up, preferred_element_type=jnp.float32).astype(
            jnp.bfloat16
        ),
        "tensor",
        scatter_dimension=0,
        tiled=True,
    ).astype(jnp.float32)
    grad_mlp_in = jnp.transpose(grad_mlp_rows, (1, 2, 0, 3))
    grad_shift_two = jnp.sum(grad_mlp_in, axis=2)
    grad_scale_two = jnp.sum(grad_mlp_in * normed_two, axis=2)
    grad_hidden = cotangent + norm_back(grad_mlp_in * (1.0 + scale_two), normed_two, inverse_two)
    grad_branch = gate_one * grad_hidden
    grad_gate_one = jnp.sum(grad_hidden * branch_one, axis=2)
    grad_b_out = jnp.sum(grad_branch, axis=(0, 1, 2))
    grad_branch_all = lax.all_gather(grad_branch.astype(jnp.bfloat16), "tensor", axis=2, tiled=True)
    grad_attended = jnp.einsum(
        "cfpd,ed->cfpe", grad_branch_all, w_out, preferred_element_type=jnp.float32
    ).astype(jnp.bfloat16)
    grad_w_out = jnp.einsum(
        "cfpe,cfpd->ed", attended_rows, grad_branch_all, preferred_element_type=jnp.float32
    )
    grad_heads = grad_attended.reshape(clip_count, block_count, block_rows, heads_local, HD)

    def backward_clip(members):
        clip_queries, keys, values, context_limit, clip_grads, clip_totals = members

        def backward_block(running, slices):
            key_acc, value_acc = running
            query_block, frames_block, grad_block, total_block = slices
            scores = masked_scores(query_block, keys, frames_block, context_limit)
            probability = jnp.exp(scores - total_block[..., None])
            grad_prob = jnp.einsum(
                "bhd,khd->hbk", grad_block, values, preferred_element_type=jnp.float32
            )
            inner_sum = jnp.sum(probability * grad_prob, axis=-1, keepdims=True)
            grad_scores = (probability * (grad_prob - inner_sum)).astype(jnp.bfloat16)
            grad_query = (
                jnp.einsum("hbk,khd->bhd", grad_scores, keys, preferred_element_type=jnp.float32)
                * softmax_scale
            )
            key_acc = (
                key_acc
                + jnp.einsum(
                    "hbk,bhd->khd", grad_scores, query_block, preferred_element_type=jnp.float32
                )
                * softmax_scale
            )
            value_acc = value_acc + jnp.einsum(
                "hbk,bhd->khd",
                probability.astype(jnp.bfloat16),
                grad_block,
                preferred_element_type=jnp.float32,
            )
            return ((key_acc, value_acc), grad_query.astype(jnp.bfloat16))

        empty_acc = jnp.zeros((key_rows, heads_local, HD), jnp.float32)
        (grad_keys, grad_values), grad_queries = lax.scan(
            backward_block,
            (empty_acc, empty_acc),
            (clip_queries, query_frames, clip_grads, clip_totals),
        )
        return (grad_queries, grad_keys, grad_values)

    grad_queries, grad_keys, grad_values = lax.map(
        backward_clip, (query_heads, key_heads, value_heads, context_frames, grad_heads, log_total)
    )
    key_shape = (clip_count, key_clip.shape[1], patches_all, head_cols)
    grad_key_own, grad_value_own = (
        lax.psum_scatter(
            grad_keys.reshape(key_shape).astype(jnp.bfloat16),
            "seq",
            scatter_dimension=1,
            tiled=True,
        ).astype(jnp.float32),
        lax.psum_scatter(
            grad_values.reshape(key_shape).astype(jnp.bfloat16),
            "seq",
            scatter_dimension=1,
            tiled=True,
        ).astype(jnp.float32),
    )
    grad_qkv = jnp.stack(
        [
            grad_queries.reshape(clip_count, half_frames, patches_all, head_cols),
            grad_key_own.astype(jnp.bfloat16),
            grad_value_own.astype(jnp.bfloat16),
        ],
        axis=3,
    )
    grad_w_qkv = jnp.einsum(
        "cfpd,cfpke->dke", attn_all, grad_qkv, preferred_element_type=jnp.float32
    )
    grad_qv_bias = jnp.sum(grad_qkv[:, :, :, 0::2, :].astype(jnp.float32), axis=(0, 1, 2))
    portion = grad_qkv
    grad_attn_rows = lax.psum_scatter(
        jnp.einsum("cfpke,dke->pcfd", portion, w_qkv, preferred_element_type=jnp.float32).astype(
            jnp.bfloat16
        ),
        "tensor",
        scatter_dimension=0,
        tiled=True,
    ).astype(jnp.float32)
    grad_attn_in = jnp.transpose(grad_attn_rows, (1, 2, 0, 3))
    grad_shift_one = jnp.sum(grad_attn_in, axis=2)
    grad_scale_one = jnp.sum(grad_attn_in * normed_one, axis=2)
    grad_input = grad_hidden + norm_back(grad_attn_in * (1.0 + scale_one), normed_one, inverse_one)
    grad_modulation = jnp.concatenate(
        [
            grad_shift_one,
            grad_scale_one,
            grad_gate_one,
            grad_shift_two,
            grad_scale_two,
            grad_gate_two,
        ],
        axis=-1,
    )
    grad_modulation = grad_modulation.reshape(clip_count * half_frames, 6 * breadth)
    modulation_cols, out_bias_part, down_bias_part = (
        lax.psum_scatter(
            grad_modulation.astype(jnp.bfloat16), "tensor", scatter_dimension=1, tiled=True
        ).astype(jnp.float32),
        lax.psum_scatter(
            grad_b_out.astype(jnp.bfloat16), "tensor", scatter_dimension=0, tiled=True
        ).astype(jnp.float32),
        lax.psum_scatter(
            grad_b_down.astype(jnp.bfloat16), "tensor", scatter_dimension=0, tiled=True
        ).astype(jnp.float32),
    )
    condition_rows = condition.reshape(clip_count * half_frames, breadth).astype(jnp.float32)
    grad_w_mod = jnp.dot(condition_rows.T, modulation_cols, precision=lax.Precision.HIGHEST)
    grad_b_mod = jnp.sum(modulation_cols, axis=0)
    (
        total_w_qkv,
        total_qv_bias,
        total_w_out,
        total_b_out,
        total_w_up,
        total_b_up,
        total_w_down,
        total_b_down,
        total_w_mod,
        total_b_mod,
    ) = (
        lax.psum(grad_w_qkv.astype(jnp.bfloat16), ("dp", "seq")).astype(jnp.float32),
        lax.psum(grad_qv_bias.astype(jnp.bfloat16), ("dp", "seq")).astype(jnp.float32),
        lax.psum(grad_w_out.astype(jnp.bfloat16), ("dp", "seq")).astype(jnp.float32),
        lax.psum(out_bias_part.astype(jnp.bfloat16), ("dp", "seq")).astype(jnp.float32),
        lax.psum(grad_w_up.astype(jnp.bfloat16), ("dp", "seq")).astype(jnp.float32),
        lax.psum(grad_b_up.astype(jnp.bfloat16), ("dp", "seq")).astype(jnp.float32),
        lax.psum(grad_w_down.astype(jnp.bfloat16), ("dp", "seq")).astype(jnp.float32),
        lax.psum(down_bias_part.astype(jnp.bfloat16), ("dp", "seq")).astype(jnp.float32),
        lax.psum(grad_w_mod.astype(jnp.bfloat16), ("dp", "seq")).astype(jnp.float32),
        lax.psum(grad_b_mod.astype(jnp.bfloat16), ("dp", "seq")).astype(jnp.float32),
    )
    return (
        output,
        grad_input,
        total_w_qkv,
        total_qv_bias,
        total_w_out,
        total_b_out,
        total_w_up,
        total_b_up,
        total_w_down,
        total_b_down,
        total_w_mod,
        total_b_mod,
    )


def solution(mesh):
    placed = (
        P("dp", "seq", "tensor", None),
        P(None, None, "tensor"),
        P(None, "tensor"),
        P("tensor", None),
        P(),
        P(None, "tensor"),
        P("tensor"),
        P("tensor", None),
        P(),
        P(),
        P(),
        P("dp"),
        P("dp", "seq"),
        P("dp", "seq", "tensor", None),
    )
    return jax.shard_map(
        body,
        mesh=mesh,
        in_specs=placed,
        out_specs=(
            P("dp", "seq", "tensor", None),
            P("dp", "seq", "tensor", None),
            P(None, None, "tensor"),
            P(None, "tensor"),
            P("tensor", None),
            P("tensor"),
            P(None, "tensor"),
            P("tensor"),
            P("tensor", None),
            P("tensor"),
            P(None, "tensor"),
            P("tensor"),
        ),
        check_vma=False,
    )
```

profile of v0, /device:TPU:0, one launch (start us, length us, event | category | flops | bytes accessed | tf_op | source)
XLA Modules:
  0.0 1632.9 jit_solution(15091767421687436867)
XLA Ops:
  21.3 83.5 %all-gather.8.cloned.1.call-done = bf16[1,8,256,1024]{3,2,1,0:T(8,128)(2,1)} async-done(((bf16[1,8,64,1024]{3,2,1,0:T(8,128)(2,1)}), bf16[1,8,256,1024]{3,2,1,0:T(8,128)(2,1)}) %all-gather.8.cloned.1.call-update) | async-done | bytes 4194320 | tf_op jit(solution)/shard_map/all_gather | solution.py:69
  147.6 198.6 %while.50 = (s32[]{:T(128)}, bf16[4,512,4,64]{1,3,2,0:T(8,128)(2,1)S(1)}, f32[4,4,512]{2,1,0:T(4,128)S(1)}, s32[4,512]{1,0:T(4,128)S(1)}, s32[]{:T(128)}, /*inde...) while((s32[]{:T(128)}, ...), condition=%wide.region_5.6_spmd.clone.clone, body=%wide.region_2.5_spmd.clone.clone.sunk | while | flops 2252539904 | bytes 122271888 | solution.py:116
  181.1 16.3 fusion.178
  199.6 16.0 fusion.176
  230.7 16.3 fusion.178
  280.3 16.3 fusion.178
  329.9 16.3 fusion.178
  354.7 76.7 %reduce-scatter.8.cloned.1.call-done = bf16[64,1,8,1024]{3,0,2,1:T(8,128)(2,1)} async-done(((bf16[256,1,8,1024]{3,0,2,1:T(8,128)(2,1)}), bf16[64,1,8,1024]{3,0,2,1:T(8,128)(2,1)}) %reduce-scatter.8.cloned.1.call-update) | async-done | bytes 1048592 | tf_op jit(solution)/shard_map/reduce_scatter | solution.py:123
  436.6 81.3 %all-gather.12.cloned.1.call-done = bf16[1,8,256,1024]{3,2,1,0:T(8,128)(2,1)} async-done(((bf16[1,8,64,1024]{3,2,1,0:T(8,128)(2,1)}), bf16[1,8,256,1024]{3,2,1,0:T(8,128)(2,1)}) %all-gather.12.cloned.1.call-update) | async-done | bytes 4194320 | tf_op jit(solution)/shard_map/all_gather | solution.py:135
  535.7 74.8 %reduce-scatter.10.cloned.1.call-done = bf16[64,1,8,1024]{3,0,2,1:T(8,128)(2,1)} async-done(((bf16[256,1,8,1024]{3,0,2,1:T(8,128)(2,1)}), bf16[64,1,8,1024]{3,0,2,1:T(8,128)(2,1)}) %reduce-scatter.10.cloned.1.call-update) | async-done | bytes 1048592 | tf_op jit(solution)/shard_map/reduce_scatter | solution.py:141
  614.5 81.4 %all-gather.14.cloned.1.call-done = bf16[1,8,256,1024]{3,2,1,0:T(8,128)(2,1)} async-done(((bf16[1,8,64,1024]{3,2,1,0:T(8,128)(2,1)}), bf16[1,8,256,1024]{3,2,1,0:T(8,128)(2,1)}) %all-gather.14.cloned.1.call-update) | async-done | bytes 4194320 | tf_op jit(solution)/shard_map/all_gather | solution.py:155
  717.5 75.4 %reduce-scatter.12.cloned.1.call-done = bf16[64,1,8,1024]{3,0,2,1:T(8,128)(2,1)} async-done(((bf16[256,1,8,1024]{3,0,2,1:T(8,128)(2,1)}), bf16[64,1,8,1024]{3,0,2,1:T(8,128)(2,1)}) %reduce-scatter.12.cloned.1.call-update) | async-done | bytes 1048592 | tf_op jit(solution)/shard_map/reduce_scatter | solution.py:164
  803.0 81.3 %all-gather.16.cloned.1.call-done = bf16[1,8,256,1024]{3,2,1,0:T(8,128)(2,1)} async-done(((bf16[1,8,64,1024]{3,2,1,0:T(8,128)(2,1)}), bf16[1,8,256,1024]{3,2,1,0:T(8,128)(2,1)}) %all-gather.16.cloned.1.call-update) | async-done | bytes 4194320 | tf_op jit(solution)/shard_map/all_gather | solution.py:179
  892.2 435.7 %while.51 = (s32[]{:T(128)}, f32[4096,4,64]{0,2,1:T(8,128)}, f32[4096,4,64]{0,2,1:T(8,128)}, bf16[4,512,4,64]{1,3,2,0:T(8,128)(2,1)}, bf16[4,512,4,64]{1,3,2,0:T...) while((s32[]{:T(128)}, f32[4096,4,64]{0,2,1:T(8,128)}, ...), condition=%wide.region_15.16_spmd.clone.clone, body=%wide.region_13.15_spmd.clone.clone.sunk | while | flops 5504305152 | bytes 351639744 | solution.py:221
  894.6 17.3 %fusion.188 = f32[4,512,4096]{2,1,0:T(8,128)} fusion(bf16[4096,4,64]{0,2,1:T(8,128)(2,1)} %get-tuple-element.645, bf16[4,512,4,64]{1,3,2,0:T(8,128)(2,1)} %get-tuple-element.642, s32[]{:T(128)S(6)} %copy.131), kind=kOutput, calls=%fused_computation.48.clone.1 | convolution fusion | flops 1073741824 | bytes 35913732 | tf_op jit(solution)/shard_map/while/body/eval_jaxpr/while/body/eval_jaxpr/bhd,khd->hbk/dot_general | solution.py:93
  911.9 16.5 %fusion.190 = f32[4096,4,64]{0,2,1:T(8,128)} fusion(f32[4,512,4096]{2,1,0:T(8,128)} %fusion.188, f32[4,512]{1,0:T(4,128)S(1)} %dynamic-slice_bitcast_fusion.2, pred[512,4096]{1,0:T(8,128)(4,1)S(1)} %compare_or_fusion.5, f32[4096,4,64]{0,2,1:T(8,128)} %get-tuple-element.627, pred[]{:T(512)S(6)} %compare.9, ...), kind=kOutput, calls=%fused_computation.39.clone.1 | convolution fusion | flops 1109393408 | bytes 44310532 | tf_op jit(solution)/shard_map/while/body/eval_jaxpr/while/body/eval_jaxpr/hbk,bhd->khd/dot_general | solution.py:212
  928.4 25.9 %multiply_reduce_fusion.6 = (f32[4,512]{1,0:T(4,128)S(1)}, f32[4,512,4096]{2,1,0:T(8,128)}) fusion(f32[4,512,4096]{2,1,0:T(8,128)} %fusion.188, f32[4,512]{1,0:T(4,128)S(1)} %dynamic-slice_bitcast_fusion.2, pred[512,4096]{1,0:T(8,128)(4,1)S(1)} %compare_or_fusion.5, bf16[4096,4,64]{0,2,1:T(8,128)(2,1)} %get-tuple-element.648, ...), kind=kOutput, calls=%fused_computation.29.clone.1 | convolution fusion | flops 1115682816 | bytes 71581696 | tf_op jit(solution)/shard_map/while/body/eval_jaxpr/while/body/eval_jaxpr/bhd,khd->hbk/dot_general | solution.py:196
  954.3 27.6 %multiply_convert_fusion.10 = bf16[4,512,4096]{2,1,0:T(8,128)(2,1)} fusion(f32[4,512,4096]{2,1,0:T(8,128)} %get-tuple-element.583, f32[4,512,4096]{2,1,0:T(8,128)} %fusion.188, f32[4,512]{1,0:T(4,128)S(1)} %get-tuple-element.584, f32[4,512]{1,0:T(4,128)S(1)} %dynamic-slice_bitcast_fusion.2, pred[512,4096]{1,0:T(8,128)(4,1)S(1)} %compare_or_fusion.5), kind=kLoop, calls=%fused_computation.28.clone.1 | loop fusion | flops 50331648 | bytes 85999616 | tf_op jit(solution)/shard_map/while/body/eval_jaxpr/while/body/eval_jaxpr/convert_element_type | solution.py:200
  1001.5 17.3 %fusion.188 = f32[4,512,4096]{2,1,0:T(8,128)} fusion(bf16[4096,4,64]{0,2,1:T(8,128)(2,1)} %get-tuple-element.645, bf16[4,512,4,64]{1,3,2,0:T(8,128)(2,1)} %get-tuple-element.642, s32[]{:T(128)S(6)} %copy.131), kind=kOutput, calls=%fused_computation.48.clone.1 | convolution fusion | flops 1073741824 | bytes 35913732 | tf_op jit(solution)/shard_map/while/body/eval_jaxpr/while/body/eval_jaxpr/bhd,khd->hbk/dot_general | solution.py:93
  1018.8 17.7 %fusion.190 = f32[4096,4,64]{0,2,1:T(8,128)} fusion(f32[4,512,4096]{2,1,0:T(8,128)} %fusion.188, f32[4,512]{1,0:T(4,128)S(1)} %dynamic-slice_bitcast_fusion.2, pred[512,4096]{1,0:T(8,128)(4,1)S(1)} %compare_or_fusion.5, f32[4096,4,64]{0,2,1:T(8,128)} %get-tuple-element.627, pred[]{:T(512)S(6)} %compare.9, ...), kind=kOutput, calls=%fused_computation.39.clone.1 | convolution fusion | flops 1109393408 | bytes 44310532 | tf_op jit(solution)/shard_map/while/body/eval_jaxpr/while/body/eval_jaxpr/hbk,bhd->khd/dot_general | solution.py:212
  1036.5 25.9 %multiply_reduce_fusion.6 = (f32[4,512]{1,0:T(4,128)S(1)}, f32[4,512,4096]{2,1,0:T(8,128)}) fusion(f32[4,512,4096]{2,1,0:T(8,128)} %fusion.188, f32[4,512]{1,0:T(4,128)S(1)} %dynamic-slice_bitcast_fusion.2, pred[512,4096]{1,0:T(8,128)(4,1)S(1)} %compare_or_fusion.5, bf16[4096,4,64]{0,2,1:T(8,128)(2,1)} %get-tuple-element.648, ...), kind=kOutput, calls=%fused_computation.29.clone.1 | convolution fusion | flops 1115682816 | bytes 71581696 | tf_op jit(solution)/shard_map/while/body/eval_jaxpr/while/body/eval_jaxpr/bhd,khd->hbk/dot_general | solution.py:196
  1062.4 27.6 %multiply_convert_fusion.10 = bf16[4,512,4096]{2,1,0:T(8,128)(2,1)} fusion(f32[4,512,4096]{2,1,0:T(8,128)} %get-tuple-element.583, f32[4,512,4096]{2,1,0:T(8,128)} %fusion.188, f32[4,512]{1,0:T(4,128)S(1)} %get-tuple-element.584, f32[4,512]{1,0:T(4,128)S(1)} %dynamic-slice_bitcast_fusion.2, pred[512,4096]{1,0:T(8,128)(4,1)S(1)} %compare_or_fusion.5), kind=kLoop, calls=%fused_computation.28.clone.1 | loop fusion | flops 50331648 | bytes 85999616 | tf_op jit(solution)/shard_map/while/body/eval_jaxpr/while/body/eval_jaxpr/convert_element_type | solution.py:200
  1110.9 17.3 %fusion.188 = f32[4,512,4096]{2,1,0:T(8,128)} fusion(bf16[4096,4,64]{0,2,1:T(8,128)(2,1)} %get-tuple-element.645, bf16[4,512,4,64]{1,3,2,0:T(8,128)(2,1)} %get-tuple-element.642, s32[]{:T(128)S(6)} %copy.131), kind=kOutput, calls=%fused_computation.48.clone.1 | convolution fusion | flops 1073741824 | bytes 35913732 | tf_op jit(solution)/shard_map/while/body/eval_jaxpr/while/body/eval_jaxpr/bhd,khd->hbk/dot_general | solution.py:93
  1128.2 17.7 %fusion.190 = f32[4096,4,64]{0,2,1:T(8,128)} fusion(f32[4,512,4096]{2,1,0:T(8,128)} %fusion.188, f32[4,512]{1,0:T(4,128)S(1)} %dynamic-slice_bitcast_fusion.2, pred[512,4096]{1,0:T(8,128)(4,1)S(1)} %compare_or_fusion.5, f32[4096,4,64]{0,2,1:T(8,128)} %get-tuple-element.627, pred[]{:T(512)S(6)} %compare.9, ...), kind=kOutput, calls=%fused_computation.39.clone.1 | convolution fusion | flops 1109393408 | bytes 44310532 | tf_op jit(solution)/shard_map/while/body/eval_jaxpr/while/body/eval_jaxpr/hbk,bhd->khd/dot_general | solution.py:212
  1145.9 25.9 %multiply_reduce_fusion.6 = (f32[4,512]{1,0:T(4,128)S(1)}, f32[4,512,4096]{2,1,0:T(8,128)}) fusion(f32[4,512,4096]{2,1,0:T(8,128)} %fusion.188, f32[4,512]{1,0:T(4,128)S(1)} %dynamic-slice_bitcast_fusion.2, pred[512,4096]{1,0:T(8,128)(4,1)S(1)} %compare_or_fusion.5, bf16[4096,4,64]{0,2,1:T(8,128)(2,1)} %get-tuple-element.648, ...), kind=kOutput, calls=%fused_computation.29.clone.1 | convolution fusion | flops 1115682816 | bytes 71581696 | tf_op jit(solution)/shard_map/while/body/eval_jaxpr/while/body/eval_jaxpr/bhd,khd->hbk/dot_general | solution.py:196
  1171.8 27.6 %multiply_convert_fusion.10 = bf16[4,512,4096]{2,1,0:T(8,128)(2,1)} fusion(f32[4,512,4096]{2,1,0:T(8,128)} %get-tuple-element.583, f32[4,512,4096]{2,1,0:T(8,128)} %fusion.188, f32[4,512]{1,0:T(4,128)S(1)} %get-tuple-element.584, f32[4,512]{1,0:T(4,128)S(1)} %dynamic-slice_bitcast_fusion.2, pred[512,4096]{1,0:T(8,128)(4,1)S(1)} %compare_or_fusion.5), kind=kLoop, calls=%fused_computation.28.clone.1 | loop fusion | flops 50331648 | bytes 85999616 | tf_op jit(solution)/shard_map/while/body/eval_jaxpr/while/body/eval_jaxpr/convert_element_type | solution.py:200
  1220.3 17.3 %fusion.188 = f32[4,512,4096]{2,1,0:T(8,128)} fusion(bf16[4096,4,64]{0,2,1:T(8,128)(2,1)} %get-tuple-element.645, bf16[4,512,4,64]{1,3,2,0:T(8,128)(2,1)} %get-tuple-element.642, s32[]{:T(128)S(6)} %copy.131), kind=kOutput, calls=%fused_computation.48.clone.1 | convolution fusion | flops 1073741824 | bytes 35913732 | tf_op jit(solution)/shard_map/while/body/eval_jaxpr/while/body/eval_jaxpr/bhd,khd->hbk/dot_general | solution.py:93
  1237.6 17.7 %fusion.190 = f32[4096,4,64]{0,2,1:T(8,128)} fusion(f32[4,512,4096]{2,1,0:T(8,128)} %fusion.188, f32[4,512]{1,0:T(4,128)S(1)} %dynamic-slice_bitcast_fusion.2, pred[512,4096]{1,0:T(8,128)(4,1)S(1)} %compare_or_fusion.5, f32[4096,4,64]{0,2,1:T(8,128)} %get-tuple-element.627, pred[]{:T(512)S(6)} %compare.9, ...), kind=kOutput, calls=%fused_computation.39.clone.1 | convolution fusion | flops 1109393408 | bytes 44310532 | tf_op jit(solution)/shard_map/while/body/eval_jaxpr/while/body/eval_jaxpr/hbk,bhd->khd/dot_general | solution.py:212
  1255.3 25.9 %multiply_reduce_fusion.6 = (f32[4,512]{1,0:T(4,128)S(1)}, f32[4,512,4096]{2,1,0:T(8,128)}) fusion(f32[4,512,4096]{2,1,0:T(8,128)} %fusion.188, f32[4,512]{1,0:T(4,128)S(1)} %dynamic-slice_bitcast_fusion.2, pred[512,4096]{1,0:T(8,128)(4,1)S(1)} %compare_or_fusion.5, bf16[4096,4,64]{0,2,1:T(8,128)(2,1)} %get-tuple-element.648, ...), kind=kOutput, calls=%fused_computation.29.clone.1 | convolution fusion | flops 1115682816 | bytes 71581696 | tf_op jit(solution)/shard_map/while/body/eval_jaxpr/while/body/eval_jaxpr/bhd,khd->hbk/dot_general | solution.py:196
  1281.2 27.6 %multiply_convert_fusion.10 = bf16[4,512,4096]{2,1,0:T(8,128)(2,1)} fusion(f32[4,512,4096]{2,1,0:T(8,128)} %get-tuple-element.583, f32[4,512,4096]{2,1,0:T(8,128)} %fusion.188, f32[4,512]{1,0:T(4,128)S(1)} %get-tuple-element.584, f32[4,512]{1,0:T(4,128)S(1)} %dynamic-slice_bitcast_fusion.2, pred[512,4096]{1,0:T(8,128)(4,1)S(1)} %compare_or_fusion.5), kind=kLoop, calls=%fused_computation.28.clone.1 | loop fusion | flops 50331648 | bytes 85999616 | tf_op jit(solution)/shard_map/while/body/eval_jaxpr/while/body/eval_jaxpr/convert_element_type | solution.py:200
  1389.7 55.0 %reduce-scatter.18.cloned.1.call-done = bf16[64,1,8,1024]{3,0,2,1:T(8,128)(2,1)} async-done(((bf16[256,1,8,1024]{3,0,2,1:T(8,128)(2,1)}), bf16[64,1,8,1024]{3,0,2,1:T(8,128)(2,1)}) %reduce-scatter.18.cloned.1.call-update) | async-done | bytes 1048592 | tf_op jit(solution)/shard_map/reduce_scatter | solution.py:259
  1504.7 106.7 %all-reduce.7.cloned.1.call-done = (bf16[1024,3,256]{2,0,1:T(8,128)(2,1)}, bf16[256,1024]{1,0:T(8,128)(2,1)}, bf16[1024,1024]{1,0:T(8,128)(2,1)}, bf16[1024,1024]{1,0:T(8,128)(2,1)}, bf16[1024,1536]{1,0:T(8,128)(2,1)}) async-done(((bf16[1024,3,256]{2,0,1:T(8,128)(2,1)}, bf16[256,1024]{1,0:T(8,128)(2,1)}, bf16[1024,1024]{1,0:T(8,128)(2,1)}, bf16[1024,1024]{1,0:T(8,128)(2,1)}, bf16[1024,1536]{1,0:T(8,128)(2,1)}), ...) | async-done | bytes 9437200 | tf_op jit(solution)/shard_map/psum | solution.py:309
  (316 shorter events, 465.0 us)
Async XLA Ops:
  7.2 520.9 %copy-start = (bf16[1024,1024]{1,0:T(8,128)(2,1)S(1)}, bf16[1024,1024]{1,0:T(8,128)(2,1)}, u32[]{:S(2)}) copy-start(bf16[1024,1024]{1,0:T(8,128)(2,1)} %param.25) | copy-start | bytes 6291460
  7.2 97.7 %all-gather.8.cloned.1.call-start = ((), (), s32[]{:S(2)}) async-start(), calls=%async_computation.7 | async-start | bytes 5242880 | tf_op jit(solution)/shard_map/all_gather | solution.py:69
  21.3 108.8 %all-gather.10.cloned.1.call-start = ((), (), s32[]{:S(2)}) async-start(), calls=%async_computation.8 | async-start | bytes 3145728 | tf_op jit(solution)/shard_map/all_gather | solution.py:77
  114.4 24.4 %all-gather.18.cloned.1.call-start = ((), (), s32[]{:S(2)}) async-start(), calls=%async_computation.19 | async-start | bytes 3145728 | tf_op jit(solution)/shard_map/all_gather | solution.py:76
  117.2 314.2 %reduce-scatter.8.cloned.1.call-start = ((), (), s32[]{:S(2)}) async-start(), calls=%async_computation.9 | async-start | bytes 5242880 | tf_op jit(solution)/shard_map/reduce_scatter | solution.py:123
  349.8 81.6 %copy-start.23 = (f32[8,1024]{1,0:T(8,128)S(1)}, f32[8,1024]{1,0:T(8,128)}, u32[]{:S(2)}) copy-start(f32[8,1024]{1,0:T(8,128)} %get-tuple-element.454) | copy-start | bytes 98308
  354.6 80.4 %copy-start.24 = (f32[8,1024]{1,0:T(8,128)S(1)}, f32[8,1024]{1,0:T(8,128)}, u32[]{:S(2)}) copy-start(f32[8,1024]{1,0:T(8,128)} %get-tuple-element.451) | copy-start | bytes 98308
  354.6 80.4 %copy-start.32 = (f32[8,1024]{1,0:T(8,128)S(1)}, f32[8,1024]{1,0:T(8,128)}, u32[]{:S(2)}) copy-start(f32[8,1024]{1,0:T(8,128)} %get-tuple-element.450) | copy-start | bytes 98308
  354.6 163.3 %all-gather.12.cloned.1.call-start = ((), (), s32[]{:S(2)}) async-start(), calls=%async_computation.10 | async-start | bytes 5242880 | tf_op jit(solution)/shard_map/all_gather | solution.py:135
  436.5 174.0 %reduce-scatter.10.cloned.1.call-start = ((), (), s32[]{:S(2)}) async-start(), calls=%async_computation.11 | async-start | bytes 5242880 | tf_op jit(solution)/shard_map/reduce_scatter | solution.py:141
  436.6 259.3 %copy-start.45 = (f32[1024]{0:T(1024)}, f32[1024]{0:T(1024)S(1)}, u32[]{:S(2)}) copy-start(f32[1024]{0:T(1024)S(1)} %convert_element_type.268) | copy-start | bytes 12292
  535.0 75.5 %copy-start.26 = (f32[8,1024]{1,0:T(8,128)S(1)}, f32[8,1024]{1,0:T(8,128)}, u32[]{:S(2)}) copy-start(f32[8,1024]{1,0:T(8,128)} %get-tuple-element.449) | copy-start | bytes 98308
  535.1 160.8 %all-gather.14.cloned.1.call-start = ((), (), s32[]{:S(2)}) async-start(), calls=%async_computation.12 | async-start | bytes 5242880 | tf_op jit(solution)/shard_map/all_gather | solution.py:155
  614.4 178.5 %reduce-scatter.12.cloned.1.call-start = ((), (), s32[]{:S(2)}) async-start(), calls=%async_computation.13 | async-start | bytes 5242880 | tf_op jit(solution)/shard_map/reduce_scatter | solution.py:164
  717.4 75.5 %copy-start.7 = (f32[1,8,64,1024]{3,2,1,0:T(8,128)S(1)}, f32[1,8,64,1024]{3,2,1,0:T(8,128)}, u32[]{:S(2)}) copy-start(f32[1,8,64,1024]{3,2,1,0:T(8,128)} %copy-done.6) | copy-start | bytes 6291460
  717.4 78.4 %copy-start.17 = (bf16[64,1,8,1024]{3,0,2,1:T(8,128)(2,1)S(1)}, bf16[64,1,8,1024]{3,0,2,1:T(8,128)(2,1)}, u32[]{:S(2)}) copy-start(bf16[64,1,8,1024]{3,0,2,1:T(8,128)(2,1)} %reduce-scatter.8.cloned.1.call-done) | copy-start | bytes 3145732
  717.5 166.9 %all-gather.16.cloned.1.call-start = ((), (), s32[]{:S(2)}) async-start(), calls=%async_computation.14 | async-start | bytes 5242880 | tf_op jit(solution)/shard_map/all_gather | solution.py:179
  800.4 84.0 %copy-start.25 = (bf16[256,1024]{1,0:T(8,128)(2,1)S(1)}, bf16[256,1024]{1,0:T(8,128)(2,1)}, u32[]{:S(2)}) copy-start(bf16[256,1024]{1,0:T(8,128)(2,1)} %param.21) | copy-start | bytes 1572868
  803.0 545.5 %reduce-scatter.14.cloned.1.call-start = ((), (), s32[]{:S(2)}) async-start(), calls=%async_computation.15 | async-start | bytes 3145728 | tf_op jit(solution)/shard_map/reduce_scatter | solution.py:233
  1336.7 22.3 %reduce-scatter.16.cloned.1.call-start = ((), (), s32[]{:S(2)}) async-start(), calls=%async_computation.16 | async-start | bytes 3145728 | tf_op jit(solution)/shard_map/reduce_scatter | solution.py:239
  1345.6 99.1 %reduce-scatter.18.cloned.1.call-start = ((), (), s32[]{:S(2)}) async-start(), calls=%async_computation.17 | async-start | bytes 5242880 | tf_op jit(solution)/shard_map/reduce_scatter | solution.py:259
  1366.6 102.9 %reduce-scatter.20.cloned.1.call-start = ((), (), s32[]{:S(2)}) async-start(), calls=%async_computation.18 | async-start | bytes 122880 | tf_op jit(solution)/shard_map/reduce_scatter | solution.py:284
  1387.6 58.6 %copy-start.5 = (f32[1,8,64,1024]{3,2,1,0:T(8,128)S(1)}, f32[1,8,64,1024]{3,2,1,0:T(8,128)}, u32[]{:S(2)}) copy-start(f32[1,8,64,1024]{3,2,1,0:T(8,128)} %param.18) | copy-start | bytes 6291460
  1387.6 58.6 %copy-start.22 = (f32[8,1024]{1,0:T(8,128)S(1)}, f32[8,1024]{1,0:T(8,128)}, u32[]{:S(2)}) copy-start(f32[8,1024]{1,0:T(8,128)} %copy-done.21) | copy-start | bytes 98308
  1387.6 58.6 %copy-start.34 = (f32[8,64]{1,0:T(8,128)S(1)}, f32[8,64]{1,0:T(8,128)}, u32[]{:S(2)}) copy-start(f32[8,64]{1,0:T(8,128)} %copy-done.33) | copy-start | bytes 6148
  1387.6 58.6 %copy-start.37 = (f32[8,64]{1,0:T(8,128)S(1)}, f32[8,64]{1,0:T(8,128)}, u32[]{:S(2)}) copy-start(f32[8,64]{1,0:T(8,128)} %copy-done.36) | copy-start | bytes 6148
  1389.7 59.0 %copy-start.40 = (bf16[8,1024]{1,0:T(8,128)(2,1)S(1)}, bf16[8,1024]{1,0:T(8,128)(2,1)}, u32[]{:S(2)}) copy-start(bf16[8,1024]{1,0:T(8,128)(2,1)} %get-tuple-element.386) | copy-start | bytes 49156
  1389.7 59.0 %copy-start.39 = (bf16[8,1024]{1,0:T(8,128)(2,1)S(1)}, bf16[8,1024]{1,0:T(8,128)(2,1)}, u32[]{:S(2)}) copy-start(bf16[8,1024]{1,0:T(8,128)(2,1)} %get-tuple-element.380) | copy-start | bytes 49156
  1389.7 59.0 %copy-start.38 = (bf16[8,1024]{1,0:T(8,128)(2,1)S(1)}, bf16[8,1024]{1,0:T(8,128)(2,1)}, u32[]{:S(2)}) copy-start(bf16[8,1024]{1,0:T(8,128)(2,1)} %get-tuple-element.384) | copy-start | bytes 49156
  1449.4 20.0 %copy-start.28 = (f32[8,512]{1,0:T(8,128)S(1)}, f32[8,512]{1,0:T(8,128)}, u32[]{:S(2)}) copy-start(f32[8,512]{1,0:T(8,128)} %copy-done.27) | copy-start | bytes 49156
  1449.5 20.0 %copy-start.30 = (f32[8,512]{1,0:T(8,128)S(1)}, f32[8,512]{1,0:T(8,128)}, u32[]{:S(2)}) copy-start(f32[8,512]{1,0:T(8,128)} %copy-done.29) | copy-start | bytes 49156
  1449.5 161.9 %all-reduce.7.cloned.1.call-start = ((), (), s32[]{:S(2)}) async-start(), calls=%async_computation.20 | async-start | bytes 18874368 | tf_op jit(solution)/shard_map/psum | solution.py:309
  (46 other events, 288.6 us)
Sparse Core Ops, SparseCore 0:
  21.4 83.4 all-gather.7
  114.6 9.0 all-gather.9
  125.8 11.7 all-gather.17
  354.7 76.6 reduce-scatter.7
  436.6 81.2 all-gather.11
  535.2 75.2 reduce-scatter.9
  614.6 81.2 all-gather.13
  717.6 75.2 reduce-scatter.11
  803.1 81.2 all-gather.15
  1336.8 8.2 reduce-scatter.13
  1347.9 11.0 reduce-scatter.15
  1366.7 78.0 reduce-scatter.17
  1449.6 19.8 reduce-scatter.19
  1474.8 136.5 all-reduce.6
where the time goes:
time: 1640 us; the launch traced here: 1630 us
  waiting for transfers between devices  739 us (45%)
  matrix products  536 us (33%)
  other arithmetic  244 us (15%)
  local copies, waits for them, and re-layouts  73.1 us (4%)
  blocking collectives  22.1 us (1%)
  between operations  16.4 us (1%)
    dot_general x8, matrix products, masked_scores(): jnp.einsum('bhd,khd->hbk', query_block, keys, preferred_element_type=jnp....  133 us
    convert_element_type x4, other arithmetic, backward_block(): grad_scores = (probability * (grad_prob - inner_sum)).astype(jnp.bfloat16)  110 us
    psum x1, waiting for transfers between devices, body(): lax.psum(grad_w_qkv.astype(jnp.bfloat16), ('dp', 'seq')).astype(jnp.float32)  107 us
    dot_general x4, matrix products, backward_block(): jnp.einsum('bhd,khd->hbk', grad_block, values, preferred_element_type=jnp...  104 us
    all_gather x1, waiting for transfers between devices, body(): attn_all = lax.all_gather(attn_in, 'tensor', axis=2, tiled=True)  83.5 us
    all_gather x1, waiting for transfers between devices, body(): grad_mlp_all = lax.all_gather(grad_mlp_low, 'tensor', axis=2, tiled=True)  81.4 us
    all_gather x1, waiting for transfers between devices, body(): mlp_all = lax.all_gather(mlp_in, 'tensor', axis=2, tiled=True)  81.3 us
    all_gather x1, waiting for transfers between devices, body(): lax.all_gather(grad_branch.astype(jnp.bfloat16), 'tensor', axis=2, tiled=...  81.3 us
  transfers between devices with their start and end apart: 14, of which 11 were waited for; matrix products, arithmetic and copies ran while one was open for 5% of the time, Pallas kernels for 0%

commit v1 on v0

--- a/solution.py
+++ b/solution.py
@@ -294,6 +294,7 @@
     condition_rows = condition.reshape(clip_count * half_frames, breadth).astype(jnp.float32)
     grad_w_mod = jnp.dot(condition_rows.T, modulation_cols, precision=lax.Precision.HIGHEST)
     grad_b_mod = jnp.sum(modulation_cols, axis=0)
+    goods_turn = lambda packet: jnp.sum(lax.all_gather(packet, ("dp", "seq")), axis=0)
     (
         total_w_qkv,
         total_qv_bias,
@@ -306,7 +307,7 @@
         total_w_mod,
         total_b_mod,
     ) = (
-        lax.psum(grad_w_qkv.astype(jnp.bfloat16), ("dp", "seq")).astype(jnp.float32),
+        goods_turn(grad_w_qkv.astype(jnp.bfloat16)).astype(jnp.float32),
         lax.psum(grad_qv_bias.astype(jnp.bfloat16), ("dp", "seq")).astype(jnp.float32),
         lax.psum(grad_w_out.astype(jnp.bfloat16), ("dp", "seq")).astype(jnp.float32),
         lax.psum(out_bias_part.astype(jnp.bfloat16), ("dp", "seq")).astype(jnp.float32),

time: 1640 us -> 1710 us (1.043)
  waiting for transfers between devices: 739 us -> 781 us
    all_gather x0 -> x1, waiting for transfers between devices: none -> 60.9 us  [body(): lax.all_gather(packet, ('dp', 'seq'))]
    psum x1, waiting for transfers between devices: 107 us -> 82.6 us  [body(): lax.psum(grad_w_out.astype(jnp.bfloat16), ('dp', 'seq')).astype(jnp.float32)]
  transfers between devices with their start and end apart: 14 -> 15, of which waited for: 11 -> 12; matrix products, arithmetic and copies ran while one was open for 5% -> 5% of each run, Pallas kernels for 0% -> 0%
where the time goes in v1:
time: 1710 us; the launch traced here: 1700 us
  waiting for transfers between devices  781 us (46%)
  matrix products  538 us (31%)
  other arithmetic  254 us (15%)
  local copies, waits for them, and re-layouts  83.5 us (5%)
  blocking collectives  22.2 us (1%)
    dot_general x8, matrix products, masked_scores(): jnp.einsum('bhd,khd->hbk', query_block, keys, preferred_element_type=jnp....  133 us
    convert_element_type x4, other arithmetic, backward_block(): grad_scores = (probability * (grad_prob - inner_sum)).astype(jnp.bfloat16)  110 us
    dot_general x4, matrix products, backward_block(): jnp.einsum('bhd,khd->hbk', grad_block, values, preferred_element_type=jnp...  104 us
    all_gather x1, waiting for transfers between devices, body(): attn_all = lax.all_gather(attn_in, 'tensor', axis=2, tiled=True)  83.5 us
    psum x1, waiting for transfers between devices, body(): lax.psum(grad_w_out.astype(jnp.bfloat16), ('dp', 'seq')).astype(jnp.float32)  82.6 us
    all_gather x1, waiting for transfers between devices, body(): grad_mlp_all = lax.all_gather(grad_mlp_low, 'tensor', axis=2, tiled=True)  81.4 us
    all_gather x1, waiting for transfers between devices, body(): lax.all_gather(grad_branch.astype(jnp.bfloat16), 'tensor', axis=2, tiled=...  81.4 us
    all_gather x1, waiting for transfers between devices, body(): mlp_all = lax.all_gather(mlp_in, 'tensor', axis=2, tiled=True)  81.3 us
  transfers between devices with their start and end apart: 15, of which 12 were waited for; matrix products, arithmetic and copies ran while one was open for 5% of the time, Pallas kernels for 0%

profile of v1, /device:TPU:0, one launch (start us, length us, event | category | flops | bytes accessed | tf_op | source)
XLA Modules:
  0.0 1696.8 jit_solution(10161964928065845031)
XLA Ops:
  21.3 83.5 %all-gather.10.cloned.1.call-done = bf16[1,8,256,1024]{3,2,1,0:T(8,128)(2,1)} async-done(((bf16[1,8,64,1024]{3,2,1,0:T(8,128)(2,1)}), bf16[1,8,256,1024]{3,2,1,0:T(8,128)(2,1)}) %all-gather.10.cloned.1.call-update) | async-done | bytes 4194320 | tf_op jit(solution)/shard_map/all_gather | solution.py:69
  147.6 198.2 %while.50 = (s32[]{:T(128)}, bf16[4,512,4,64]{1,3,2,0:T(8,128)(2,1)S(1)}, f32[4,4,512]{2,1,0:T(4,128)S(1)}, s32[4,512]{1,0:T(4,128)S(1)}, s32[]{:T(128)}, /*inde...) while((s32[]{:T(128)}, ...), condition=%wide.region_5.6_spmd.clone.clone, body=%wide.region_2.5_spmd.clone.clone.sunk | while | flops 2252539904 | bytes 122271888 | solution.py:116
  181.1 16.3 fusion.178
  230.5 16.3 fusion.178
  280.0 16.3 fusion.178
  329.5 16.3 fusion.178
  365.4 76.7 %reduce-scatter.8.cloned.1.call-done = bf16[64,1,8,1024]{3,0,2,1:T(8,128)(2,1)} async-done(((bf16[256,1,8,1024]{3,0,2,1:T(8,128)(2,1)}), bf16[64,1,8,1024]{3,0,2,1:T(8,128)(2,1)}) %reduce-scatter.8.cloned.1.call-update) | async-done | bytes 1048592 | tf_op jit(solution)/shard_map/reduce_scatter | solution.py:123
  447.3 81.3 %all-gather.14.cloned.1.call-done = bf16[1,8,256,1024]{3,2,1,0:T(8,128)(2,1)} async-done(((bf16[1,8,64,1024]{3,2,1,0:T(8,128)(2,1)}), bf16[1,8,256,1024]{3,2,1,0:T(8,128)(2,1)}) %all-gather.14.cloned.1.call-update) | async-done | bytes 4194320 | tf_op jit(solution)/shard_map/all_gather | solution.py:135
  546.4 74.8 %reduce-scatter.10.cloned.1.call-done = bf16[64,1,8,1024]{3,0,2,1:T(8,128)(2,1)} async-done(((bf16[256,1,8,1024]{3,0,2,1:T(8,128)(2,1)}), bf16[64,1,8,1024]{3,0,2,1:T(8,128)(2,1)}) %reduce-scatter.10.cloned.1.call-update) | async-done | bytes 1048592 | tf_op jit(solution)/shard_map/reduce_scatter | solution.py:141
  625.2 81.4 %all-gather.16.cloned.1.call-done = bf16[1,8,256,1024]{3,2,1,0:T(8,128)(2,1)} async-done(((bf16[1,8,64,1024]{3,2,1,0:T(8,128)(2,1)}), bf16[1,8,256,1024]{3,2,1,0:T(8,128)(2,1)}) %all-gather.16.cloned.1.call-update) | async-done | bytes 4194320 | tf_op jit(solution)/shard_map/all_gather | solution.py:155
  728.2 75.4 %reduce-scatter.12.cloned.1.call-done = bf16[64,1,8,1024]{3,0,2,1:T(8,128)(2,1)} async-done(((bf16[256,1,8,1024]{3,0,2,1:T(8,128)(2,1)}), bf16[64,1,8,1024]{3,0,2,1:T(8,128)(2,1)}) %reduce-scatter.12.cloned.1.call-update) | async-done | bytes 1048592 | tf_op jit(solution)/shard_map/reduce_scatter | solution.py:164
  813.7 81.4 %all-gather.18.cloned.1.call-done = bf16[1,8,256,1024]{3,2,1,0:T(8,128)(2,1)} async-done(((bf16[1,8,64,1024]{3,2,1,0:T(8,128)(2,1)}), bf16[1,8,256,1024]{3,2,1,0:T(8,128)(2,1)}) %all-gather.18.cloned.1.call-update) | async-done | bytes 4194320 | tf_op jit(solution)/shard_map/all_gather | solution.py:179
  902.8 435.5 %while.51 = (s32[]{:T(128)}, f32[4096,4,64]{0,2,1:T(8,128)}, f32[4096,4,64]{0,2,1:T(8,128)}, bf16[4,512,4,64]{1,3,2,0:T(8,128)(2,1)}, bf16[4,512,4,64]{1,3,2,0:T...) while((s32[]{:T(128)}, f32[4096,4,64]{0,2,1:T(8,128)}, ...), condition=%wide.region_15.16_spmd.clone.clone, body=%wide.region_13.15_spmd.clone.clone.sunk | while | flops 5504305152 | bytes 351639744 | solution.py:221
  905.4 17.3 %fusion.188 = f32[4,512,4096]{2,1,0:T(8,128)} fusion(bf16[4096,4,64]{0,2,1:T(8,128)(2,1)} %get-tuple-element.644, bf16[4,512,4,64]{1,3,2,0:T(8,128)(2,1)} %get-tuple-element.641, s32[]{:T(128)S(6)} %copy.131), kind=kOutput, calls=%fused_computation.48.clone.1 | convolution fusion | flops 1073741824 | bytes 35913732 | tf_op jit(solution)/shard_map/while/body/eval_jaxpr/while/body/eval_jaxpr/bhd,khd->hbk/dot_general | solution.py:93
  922.7 16.5 fusion.190
  939.2 25.9 %multiply_reduce_fusion.6 = (f32[4,512]{1,0:T(4,128)S(1)}, f32[4,512,4096]{2,1,0:T(8,128)}) fusion(f32[4,512,4096]{2,1,0:T(8,128)} %fusion.188, f32[4,512]{1,0:T(4,128)S(1)} %dynamic-slice_bitcast_fusion.2, pred[512,4096]{1,0:T(8,128)(4,1)S(1)} %compare_or_fusion.5, bf16[4096,4,64]{0,2,1:T(8,128)(2,1)} %get-tuple-element.647, ...), kind=kOutput, calls=%fused_computation.29.clone.1 | convolution fusion | flops 1115682816 | bytes 71581696 | tf_op jit(solution)/shard_map/while/body/eval_jaxpr/while/body/eval_jaxpr/bhd,khd->hbk/dot_general | solution.py:196
  965.1 27.6 %multiply_convert_fusion.10 = bf16[4,512,4096]{2,1,0:T(8,128)(2,1)} fusion(f32[4,512,4096]{2,1,0:T(8,128)} %get-tuple-element.582, f32[4,512,4096]{2,1,0:T(8,128)} %fusion.188, f32[4,512]{1,0:T(4,128)S(1)} %get-tuple-element.583, f32[4,512]{1,0:T(4,128)S(1)} %dynamic-slice_bitcast_fusion.2, pred[512,4096]{1,0:T(8,128)(4,1)S(1)} %compare_or_fusion.5), kind=kLoop, calls=%fused_computation.28.clone.1 | loop fusion | flops 50331648 | bytes 85999616 | tf_op jit(solution)/shard_map/while/body/eval_jaxpr/while/body/eval_jaxpr/convert_element_type | solution.py:200
  1012.3 17.3 %fusion.188 = f32[4,512,4096]{2,1,0:T(8,128)} fusion(bf16[4096,4,64]{0,2,1:T(8,128)(2,1)} %get-tuple-element.644, bf16[4,512,4,64]{1,3,2,0:T(8,128)(2,1)} %get-tuple-element.641, s32[]{:T(128)S(6)} %copy.131), kind=kOutput, calls=%fused_computation.48.clone.1 | convolution fusion | flops 1073741824 | bytes 35913732 | tf_op jit(solution)/shard_map/while/body/eval_jaxpr/while/body/eval_jaxpr/bhd,khd->hbk/dot_general | solution.py:93
  1029.6 17.7 %fusion.190 = f32[4096,4,64]{0,2,1:T(8,128)} fusion(f32[4,512,4096]{2,1,0:T(8,128)} %fusion.188, f32[4,512]{1,0:T(4,128)S(1)} %dynamic-slice_bitcast_fusion.2, pred[512,4096]{1,0:T(8,128)(4,1)S(1)} %compare_or_fusion.5, f32[4096,4,64]{0,2,1:T(8,128)} %get-tuple-element.626, pred[]{:T(512)S(6)} %compare.9, ...), kind=kOutput, calls=%fused_computation.39.clone.1 | convolution fusion | flops 1109393408 | bytes 44310532 | tf_op jit(solution)/shard_map/while/body/eval_jaxpr/while/body/eval_jaxpr/hbk,bhd->khd/dot_general | solution.py:212
  1047.3 25.9 %multiply_reduce_fusion.6 = (f32[4,512]{1,0:T(4,128)S(1)}, f32[4,512,4096]{2,1,0:T(8,128)}) fusion(f32[4,512,4096]{2,1,0:T(8,128)} %fusion.188, f32[4,512]{1,0:T(4,128)S(1)} %dynamic-slice_bitcast_fusion.2, pred[512,4096]{1,0:T(8,128)(4,1)S(1)} %compare_or_fusion.5, bf16[4096,4,64]{0,2,1:T(8,128)(2,1)} %get-tuple-element.647, ...), kind=kOutput, calls=%fused_computation.29.clone.1 | convolution fusion | flops 1115682816 | bytes 71581696 | tf_op jit(solution)/shard_map/while/body/eval_jaxpr/while/body/eval_jaxpr/bhd,khd->hbk/dot_general | solution.py:196
  1073.2 27.6 %multiply_convert_fusion.10 = bf16[4,512,4096]{2,1,0:T(8,128)(2,1)} fusion(f32[4,512,4096]{2,1,0:T(8,128)} %get-tuple-element.582, f32[4,512,4096]{2,1,0:T(8,128)} %fusion.188, f32[4,512]{1,0:T(4,128)S(1)} %get-tuple-element.583, f32[4,512]{1,0:T(4,128)S(1)} %dynamic-slice_bitcast_fusion.2, pred[512,4096]{1,0:T(8,128)(4,1)S(1)} %compare_or_fusion.5), kind=kLoop, calls=%fused_computation.28.clone.1 | loop fusion | flops 50331648 | bytes 85999616 | tf_op jit(solution)/shard_map/while/body/eval_jaxpr/while/body/eval_jaxpr/convert_element_type | solution.py:200
  1121.7 17.3 %fusion.188 = f32[4,512,4096]{2,1,0:T(8,128)} fusion(bf16[4096,4,64]{0,2,1:T(8,128)(2,1)} %get-tuple-element.644, bf16[4,512,4,64]{1,3,2,0:T(8,128)(2,1)} %get-tuple-element.641, s32[]{:T(128)S(6)} %copy.131), kind=kOutput, calls=%fused_computation.48.clone.1 | convolution fusion | flops 1073741824 | bytes 35913732 | tf_op jit(solution)/shard_map/while/body/eval_jaxpr/while/body/eval_jaxpr/bhd,khd->hbk/dot_general | solution.py:93
  1139.0 17.7 %fusion.190 = f32[4096,4,64]{0,2,1:T(8,128)} fusion(f32[4,512,4096]{2,1,0:T(8,128)} %fusion.188, f32[4,512]{1,0:T(4,128)S(1)} %dynamic-slice_bitcast_fusion.2, pred[512,4096]{1,0:T(8,128)(4,1)S(1)} %compare_or_fusion.5, f32[4096,4,64]{0,2,1:T(8,128)} %get-tuple-element.626, pred[]{:T(512)S(6)} %compare.9, ...), kind=kOutput, calls=%fused_computation.39.clone.1 | convolution fusion | flops 1109393408 | bytes 44310532 | tf_op jit(solution)/shard_map/while/body/eval_jaxpr/while/body/eval_jaxpr/hbk,bhd->khd/dot_general | solution.py:212
  1156.7 25.9 %multiply_reduce_fusion.6 = (f32[4,512]{1,0:T(4,128)S(1)}, f32[4,512,4096]{2,1,0:T(8,128)}) fusion(f32[4,512,4096]{2,1,0:T(8,128)} %fusion.188, f32[4,512]{1,0:T(4,128)S(1)} %dynamic-slice_bitcast_fusion.2, pred[512,4096]{1,0:T(8,128)(4,1)S(1)} %compare_or_fusion.5, bf16[4096,4,64]{0,2,1:T(8,128)(2,1)} %get-tuple-element.647, ...), kind=kOutput, calls=%fused_computation.29.clone.1 | convolution fusion | flops 1115682816 | bytes 71581696 | tf_op jit(solution)/shard_map/while/body/eval_jaxpr/while/body/eval_jaxpr/bhd,khd->hbk/dot_general | solution.py:196
  1182.6 27.6 %multiply_convert_fusion.10 = bf16[4,512,4096]{2,1,0:T(8,128)(2,1)} fusion(f32[4,512,4096]{2,1,0:T(8,128)} %get-tuple-element.582, f32[4,512,4096]{2,1,0:T(8,128)} %fusion.188, f32[4,512]{1,0:T(4,128)S(1)} %get-tuple-element.583, f32[4,512]{1,0:T(4,128)S(1)} %dynamic-slice_bitcast_fusion.2, pred[512,4096]{1,0:T(8,128)(4,1)S(1)} %compare_or_fusion.5), kind=kLoop, calls=%fused_computation.28.clone.1 | loop fusion | flops 50331648 | bytes 85999616 | tf_op jit(solution)/shard_map/while/body/eval_jaxpr/while/body/eval_jaxpr/convert_element_type | solution.py:200
  1231.0 17.3 %fusion.188 = f32[4,512,4096]{2,1,0:T(8,128)} fusion(bf16[4096,4,64]{0,2,1:T(8,128)(2,1)} %get-tuple-element.644, bf16[4,512,4,64]{1,3,2,0:T(8,128)(2,1)} %get-tuple-element.641, s32[]{:T(128)S(6)} %copy.131), kind=kOutput, calls=%fused_computation.48.clone.1 | convolution fusion | flops 1073741824 | bytes 35913732 | tf_op jit(solution)/shard_map/while/body/eval_jaxpr/while/body/eval_jaxpr/bhd,khd->hbk/dot_general | solution.py:93
  1248.3 17.7 %fusion.190 = f32[4096,4,64]{0,2,1:T(8,128)} fusion(f32[4,512,4096]{2,1,0:T(8,128)} %fusion.188, f32[4,512]{1,0:T(4,128)S(1)} %dynamic-slice_bitcast_fusion.2, pred[512,4096]{1,0:T(8,128)(4,1)S(1)} %compare_or_fusion.5, f32[4096,4,64]{0,2,1:T(8,128)} %get-tuple-element.626, pred[]{:T(512)S(6)} %compare.9, ...), kind=kOutput, calls=%fused_computation.39.clone.1 | convolution fusion | flops 1109393408 | bytes 44310532 | tf_op jit(solution)/shard_map/while/body/eval_jaxpr/while/body/eval_jaxpr/hbk,bhd->khd/dot_general | solution.py:212
  1266.0 25.9 %multiply_reduce_fusion.6 = (f32[4,512]{1,0:T(4,128)S(1)}, f32[4,512,4096]{2,1,0:T(8,128)}) fusion(f32[4,512,4096]{2,1,0:T(8,128)} %fusion.188, f32[4,512]{1,0:T(4,128)S(1)} %dynamic-slice_bitcast_fusion.2, pred[512,4096]{1,0:T(8,128)(4,1)S(1)} %compare_or_fusion.5, bf16[4096,4,64]{0,2,1:T(8,128)(2,1)} %get-tuple-element.647, ...), kind=kOutput, calls=%fused_computation.29.clone.1 | convolution fusion | flops 1115682816 | bytes 71581696 | tf_op jit(solution)/shard_map/while/body/eval_jaxpr/while/body/eval_jaxpr/bhd,khd->hbk/dot_general | solution.py:196
  1292.0 27.6 %multiply_convert_fusion.10 = bf16[4,512,4096]{2,1,0:T(8,128)(2,1)} fusion(f32[4,512,4096]{2,1,0:T(8,128)} %get-tuple-element.582, f32[4,512,4096]{2,1,0:T(8,128)} %fusion.188, f32[4,512]{1,0:T(4,128)S(1)} %get-tuple-element.583, f32[4,512]{1,0:T(4,128)S(1)} %dynamic-slice_bitcast_fusion.2, pred[512,4096]{1,0:T(8,128)(4,1)S(1)} %compare_or_fusion.5), kind=kLoop, calls=%fused_computation.28.clone.1 | loop fusion | flops 50331648 | bytes 85999616 | tf_op jit(solution)/shard_map/while/body/eval_jaxpr/while/body/eval_jaxpr/convert_element_type | solution.py:200
  1397.9 57.3 %reduce-scatter.18.cloned.1.call-done = bf16[64,1,8,1024]{3,0,2,1:T(8,128)(2,1)} async-done(((bf16[256,1,8,1024]{3,0,2,1:T(8,128)(2,1)}), bf16[64,1,8,1024]{3,0,2,1:T(8,128)(2,1)}) %reduce-scatter.18.cloned.1.call-update) | async-done | bytes 1048592 | tf_op jit(solution)/shard_map/reduce_scatter | solution.py:259
  1522.0 82.6 %all-reduce.7.cloned.1.call-done = (bf16[256,1024]{1,0:T(8,128)(2,1)}, bf16[1024,1024]{1,0:T(8,128)(2,1)}, bf16[1024,1024]{1,0:T(8,128)(2,1)}, bf16[1024,1536]{1,0:T(8,128)(2,1)}) async-done(((bf16[256,1024]{1,0:T(8,128)(2,1)}, bf16[1024,1024]{1,0:T(8,128)(2,1)}, bf16[1024,1024]{1,0:T(8,128)(2,1)}, bf16[1024,1536]{1,0:T(8,128)(2,1)}), (bf16[256,1024]{1,0:T(8,128)(2,1)}, bf16[1024,1024]{1,0:T(8,128)(2,1)}, ...) | async-done | bytes 7864336 | tf_op jit(solution)/shard_map/psum | solution.py:312
  1617.7 60.9 %all-gather.22.cloned.1.call-done = bf16[8192,3,256]{2,0,1:T(8,128)(2,1)} async-done(((bf16[1024,3,256]{2,0,1:T(8,128)(2,1)}), bf16[8192,3,256]{2,0,1:T(8,128)(2,1)}) %all-gather.22.cloned.1.call-update) | async-done | bytes 12582928 | tf_op jit(solution)/shard_map/all_gather | solution.py:297
  (314 shorter events, 505.8 us)
Async XLA Ops:
  7.2 531.6 %copy-start = (bf16[1024,1024]{1,0:T(8,128)(2,1)S(1)}, bf16[1024,1024]{1,0:T(8,128)(2,1)}, u32[]{:S(2)}) copy-start(bf16[1024,1024]{1,0:T(8,128)(2,1)} %param.25) | copy-start | bytes 6291460
  7.2 97.7 %all-gather.10.cloned.1.call-start = ((), (), s32[]{:S(2)}) async-start(), calls=%async_computation.7 | async-start | bytes 5242880 | tf_op jit(solution)/shard_map/all_gather | solution.py:69
  21.2 108.8 %all-gather.12.cloned.1.call-start = ((), (), s32[]{:S(2)}) async-start(), calls=%async_computation.8 | async-start | bytes 3145728 | tf_op jit(solution)/shard_map/all_gather | solution.py:77
  114.4 24.4 %all-gather.20.cloned.1.call-start = ((), (), s32[]{:S(2)}) async-start(), calls=%async_computation.19 | async-start | bytes 3145728 | tf_op jit(solution)/shard_map/all_gather | solution.py:76
  117.2 324.9 %reduce-scatter.8.cloned.1.call-start = ((), (), s32[]{:S(2)}) async-start(), calls=%async_computation.9 | async-start | bytes 5242880 | tf_op jit(solution)/shard_map/reduce_scatter | solution.py:123
  360.5 81.6 %copy-start.21 = (f32[8,1024]{1,0:T(8,128)S(1)}, f32[8,1024]{1,0:T(8,128)}, u32[]{:S(2)}) copy-start(f32[8,1024]{1,0:T(8,128)} %get-tuple-element.453) | copy-start | bytes 98308
  365.3 80.4 %copy-start.22 = (f32[8,1024]{1,0:T(8,128)S(1)}, f32[8,1024]{1,0:T(8,128)}, u32[]{:S(2)}) copy-start(f32[8,1024]{1,0:T(8,128)} %get-tuple-element.450) | copy-start | bytes 98308
  365.3 80.4 %copy-start.30 = (f32[8,1024]{1,0:T(8,128)S(1)}, f32[8,1024]{1,0:T(8,128)}, u32[]{:S(2)}) copy-start(f32[8,1024]{1,0:T(8,128)} %get-tuple-element.449) | copy-start | bytes 98308
  365.3 163.3 %all-gather.14.cloned.1.call-start = ((), (), s32[]{:S(2)}) async-start(), calls=%async_computation.10 | async-start | bytes 5242880 | tf_op jit(solution)/shard_map/all_gather | solution.py:135
  447.2 174.0 %reduce-scatter.10.cloned.1.call-start = ((), (), s32[]{:S(2)}) async-start(), calls=%async_computation.11 | async-start | bytes 5242880 | tf_op jit(solution)/shard_map/reduce_scatter | solution.py:141
  447.3 259.3 %copy-start.43 = (f32[1024]{0:T(1024)}, f32[1024]{0:T(1024)S(1)}, u32[]{:S(2)}) copy-start(f32[1024]{0:T(1024)S(1)} %convert_element_type.270) | copy-start | bytes 12292
  545.7 75.5 %copy-start.24 = (f32[8,1024]{1,0:T(8,128)S(1)}, f32[8,1024]{1,0:T(8,128)}, u32[]{:S(2)}) copy-start(f32[8,1024]{1,0:T(8,128)} %get-tuple-element.448) | copy-start | bytes 98308
  545.7 160.8 %all-gather.16.cloned.1.call-start = ((), (), s32[]{:S(2)}) async-start(), calls=%async_computation.12 | async-start | bytes 5242880 | tf_op jit(solution)/shard_map/all_gather | solution.py:155
  625.1 178.4 %reduce-scatter.12.cloned.1.call-start = ((), (), s32[]{:S(2)}) async-start(), calls=%async_computation.13 | async-start | bytes 5242880 | tf_op jit(solution)/shard_map/reduce_scatter | solution.py:164
  728.1 75.4 %copy-start.7 = (f32[1,8,64,1024]{3,2,1,0:T(8,128)S(1)}, f32[1,8,64,1024]{3,2,1,0:T(8,128)}, u32[]{:S(2)}) copy-start(f32[1,8,64,1024]{3,2,1,0:T(8,128)} %copy-done.6) | copy-start | bytes 6291460
  728.1 78.4 %copy-start.16 = (bf16[64,1,8,1024]{3,0,2,1:T(8,128)(2,1)S(1)}, bf16[64,1,8,1024]{3,0,2,1:T(8,128)(2,1)}, u32[]{:S(2)}) copy-start(bf16[64,1,8,1024]{3,0,2,1:T(8,128)(2,1)} %reduce-scatter.8.cloned.1.call-done) | copy-start | bytes 3145732
  728.1 166.9 %all-gather.18.cloned.1.call-start = ((), (), s32[]{:S(2)}) async-start(), calls=%async_computation.14 | async-start | bytes 5242880 | tf_op jit(solution)/shard_map/all_gather | solution.py:179
  811.0 84.0 %copy-start.23 = (bf16[256,1024]{1,0:T(8,128)(2,1)S(1)}, bf16[256,1024]{1,0:T(8,128)(2,1)}, u32[]{:S(2)}) copy-start(bf16[256,1024]{1,0:T(8,128)(2,1)} %param.21) | copy-start | bytes 1572868
  813.6 545.4 %reduce-scatter.14.cloned.1.call-start = ((), (), s32[]{:S(2)}) async-start(), calls=%async_computation.15 | async-start | bytes 3145728 | tf_op jit(solution)/shard_map/reduce_scatter | solution.py:233
  1347.2 22.3 %reduce-scatter.16.cloned.1.call-start = ((), (), s32[]{:S(2)}) async-start(), calls=%async_computation.16 | async-start | bytes 3145728 | tf_op jit(solution)/shard_map/reduce_scatter | solution.py:239
  1356.1 99.1 %reduce-scatter.18.cloned.1.call-start = ((), (), s32[]{:S(2)}) async-start(), calls=%async_computation.17 | async-start | bytes 5242880 | tf_op jit(solution)/shard_map/reduce_scatter | solution.py:259
  1377.0 102.7 %reduce-scatter.20.cloned.1.call-start = ((), (), s32[]{:S(2)}) async-start(), calls=%async_computation.18 | async-start | bytes 122880 | tf_op jit(solution)/shard_map/reduce_scatter | solution.py:284
  1386.6 70.1 %copy-start.5 = (f32[1,8,64,1024]{3,2,1,0:T(8,128)S(1)}, f32[1,8,64,1024]{3,2,1,0:T(8,128)}, u32[]{:S(2)}) copy-start(f32[1,8,64,1024]{3,2,1,0:T(8,128)} %param.18) | copy-start | bytes 6291460
  1386.6 70.1 %copy-start.20 = (f32[8,1024]{1,0:T(8,128)S(1)}, f32[8,1024]{1,0:T(8,128)}, u32[]{:S(2)}) copy-start(f32[8,1024]{1,0:T(8,128)} %copy-done.19) | copy-start | bytes 98308
  1386.6 70.1 %copy-start.32 = (f32[8,64]{1,0:T(8,128)S(1)}, f32[8,64]{1,0:T(8,128)}, u32[]{:S(2)}) copy-start(f32[8,64]{1,0:T(8,128)} %copy-done.31) | copy-start | bytes 6148
  1386.6 70.1 %copy-start.35 = (f32[8,64]{1,0:T(8,128)S(1)}, f32[8,64]{1,0:T(8,128)}, u32[]{:S(2)}) copy-start(f32[8,64]{1,0:T(8,128)} %copy-done.34) | copy-start | bytes 6148
  1397.7 61.3 %copy-start.38 = (bf16[8,1024]{1,0:T(8,128)(2,1)S(1)}, bf16[8,1024]{1,0:T(8,128)(2,1)}, u32[]{:S(2)}) copy-start(bf16[8,1024]{1,0:T(8,128)(2,1)} %get-tuple-element.386) | copy-start | bytes 49156
  1397.7 61.3 %copy-start.37 = (bf16[8,1024]{1,0:T(8,128)(2,1)S(1)}, bf16[8,1024]{1,0:T(8,128)(2,1)}, u32[]{:S(2)}) copy-start(bf16[8,1024]{1,0:T(8,128)(2,1)} %get-tuple-element.380) | copy-start | bytes 49156
  1397.7 61.4 %copy-start.36 = (bf16[8,1024]{1,0:T(8,128)(2,1)S(1)}, bf16[8,1024]{1,0:T(8,128)(2,1)}, u32[]{:S(2)}) copy-start(bf16[8,1024]{1,0:T(8,128)(2,1)} %get-tuple-element.384) | copy-start | bytes 49156
  1459.7 20.0 %copy-start.26 = (f32[8,512]{1,0:T(8,128)S(1)}, f32[8,512]{1,0:T(8,128)}, u32[]{:S(2)}) copy-start(f32[8,512]{1,0:T(8,128)} %copy-done.25) | copy-start | bytes 49156
  1459.7 144.9 %all-reduce.7.cloned.1.call-start = ((), (), s32[]{:S(2)}) async-start(), calls=%async_computation.21 | async-start | bytes 15728640 | tf_op jit(solution)/shard_map/psum | solution.py:312
  1483.2 195.3 %all-gather.22.cloned.1.call-start = ((), (), s32[]{:S(2)}) async-start(), calls=%async_computation.20 | async-start | bytes 14155776 | tf_op jit(solution)/shard_map/all_gather | solution.py:297
  (44 other events, 311.9 us)
Sparse Core Ops, SparseCore 0:
  21.4 83.4 all-gather.9
  114.6 9.0 all-gather.11
  125.8 11.7 all-gather.19
  365.4 76.6 reduce-scatter.7
  447.3 81.2 all-gather.13
  545.9 75.2 reduce-scatter.9
  625.2 81.2 all-gather.15
  728.3 75.2 reduce-scatter.11
  813.7 81.2 all-gather.17
  1347.3 8.2 reduce-scatter.13
  1358.4 11.0 reduce-scatter.15
  1377.1 78.0 reduce-scatter.17
  1459.8 19.8 reduce-scatter.19
  1484.5 120.1 all-reduce.6
  1606.4 72.1 all-gather.21
